TPU v7x, 32 devices: a whole 2x2x4 slice. The times are simulated.
32 devices in a mesh: ctx: 8 (over y, x, core), fsdp: 4 (over z).
Axes of the slice: x: 2, y: 2, z: 4, core: 2. Of those that a mesh axis runs over, the one named last changes fastest.
Arguments:
- tokens: bfloat16 [4, 4096, 768], P('fsdp', 'ctx'), may hold values from -6 to 6
- cotangent: bfloat16 [4, 4096, 768], P('fsdp', 'ctx'), may hold values from -6 to 6
- lengths: int32 [4, 4], P('fsdp'), may hold values from 1 to 2048, 4096 in all within a row
- dealing: int32 [4, 16], P('fsdp'), may hold values from 0 to 15, each once within a row
- qkv_weight: bfloat16 [768, 2304], P('fsdp'), may hold values from -0.21875 to 0.21875
- out_weight: bfloat16 [768, 768], P('fsdp'), may hold values from -0.21875 to 0.21875
- in_weight: bfloat16 [768, 3072], P('fsdp'), may hold values from -0.21875 to 0.21875
- back_weight: bfloat16 [3072, 768], P('fsdp'), may hold values from -0.109375 to 0.109375
- norm_gains: bfloat16 [3, 768], P(None, 'fsdp'), may hold values from 0.25 to 1.75
- shifts: bfloat16 [7, 768], P(None, 'fsdp'), may hold values from -1.796875 to 1.796875
- ffn_gain: bfloat16 [3072], P('fsdp'), may hold values from 0.25 to 1.75
- ffn_shifts: bfloat16 [2, 3072], P(None, 'fsdp'), may hold values from -1.796875 to 1.796875
Outputs:
- mixed_out: bfloat16 [4, 4096, 768], P('fsdp', 'ctx')
- input_grad: float32 [4, 4096, 768], P('fsdp', 'ctx')
- qkv_grad: float32 [768, 2304], P(('ctx', 'fsdp'))
- out_grad: float32 [768, 768], P(('ctx', 'fsdp'))
- in_grad: float32 [768, 3072], P(('ctx', 'fsdp'))
- back_grad: float32 [3072, 768], P(('ctx', 'fsdp'))
- gains_grad: float32 [3, 768], P(None, ('ctx', 'fsdp'))
- shifts_grad: float32 [7, 768], P(None, ('ctx', 'fsdp'))
- ffn_gain_grad: float32 [3072], P(('ctx', 'fsdp'))
- ffn_shifts_grad: float32 [2, 3072], P(None, ('ctx', 'fsdp'))
Inputs may be any that keep to these rules, and one draw needn't show every extreme that they name: `lengths`: each row sums to 4096 and its largest entry is exactly 2048. `dealing`: each row is a permutation of the group numbers.
All inputs are finite; a program needn't handle non-finite values.
Results may differ from a plain program's by a relative error of at most 0.018.
Values may be sent and summed in bfloat16 or wider, within the bound.
No kernel may reach another device: no remote copies, remote signals or barrier semaphores. Data moves between devices by JAX's collectives and lax.ppermute only.
A program may use at most 256 MiB of HBM per device.

v0:
```python
import math
import jax
import jax.numpy as jnp
from jax import lax
from jax.sharding import PartitionSpec as P

D = 768
H = 12
DH = 64


def layer_norm(values, gain, shift):
    average = jnp.mean(values, axis=-1, keepdims=True)
    centred = values - average
    variance = jnp.mean(centred * centred, axis=-1, keepdims=True)
    return centred * lax.rsqrt(variance + 1e-05) * gain + shift


def gelu_exact(values):
    return jax.nn.gelu(values, approximate=False)


def row_places(first_row, row_count, deal_row, bounds, group_rows):
    row_ids = first_row + jnp.arange(row_count, dtype=jnp.int32)
    group_ids = row_ids // group_rows
    onehot = (group_ids[:, None] == jnp.arange(deal_row.shape[0], dtype=jnp.int32)[None, :]).astype(
        jnp.int32
    )
    picked = jnp.sum(onehot * deal_row[None, :], axis=1)
    places = picked * group_rows + row_ids % group_rows
    segment = jnp.sum((places[:, None] >= bounds[None, :]).astype(jnp.int32), axis=1)
    return (places, segment)


def outer_sum(left, right):
    return lax.dot_general(
        left, right, (((0,), (0,)), ((), ())), preferred_element_type=jnp.float32
    )


def times_transposed(left, matrix):
    return lax.dot_general(
        left, matrix, (((1,), (1,)), ((), ())), preferred_element_type=jnp.float32
    )


def unpack(loaded):
    qkv_w, out_w, in_w, back_w, gains, shift_rows, ffn_gain, ffn_shift_rows = loaded
    return (
        qkv_w,
        out_w,
        in_w,
        back_w,
        gains.astype(jnp.float32),
        shift_rows.astype(jnp.float32),
        ffn_gain.astype(jnp.float32),
        ffn_shift_rows.astype(jnp.float32),
    )


def local(
    tokens,
    cotangent,
    lengths,
    dealing,
    qkv_weight,
    out_weight,
    in_weight,
    back_weight,
    norm_gains,
    shifts,
    ffn_gain,
    ffn_shifts,
):
    position = lax.axis_index("ctx")
    tok_rows = tokens.shape[1]
    group_rows = tok_rows // 2
    deal_row = dealing[0]
    bounds = jnp.cumsum(lengths[0])
    scaling = DH ** (-0.5)
    loaded = (
        lax.all_gather(qkv_weight, "fsdp", axis=0, tiled=True),
        lax.all_gather(out_weight, "fsdp", axis=0, tiled=True),
        lax.all_gather(in_weight, "fsdp", axis=0, tiled=True),
        lax.all_gather(back_weight, "fsdp", axis=0, tiled=True),
        lax.all_gather(norm_gains, "fsdp", axis=1, tiled=True),
        lax.all_gather(shifts, "fsdp", axis=1, tiled=True),
        lax.all_gather(ffn_gain, "fsdp", axis=0, tiled=True),
        lax.all_gather(ffn_shifts, "fsdp", axis=1, tiled=True),
    )
    qkv_w, out_w, in_w, back_w, gains, shift_rows, ffn_scale, ffn_shift_rows = unpack(loaded)
    inputs = tokens[0].astype(jnp.float32)
    normed = layer_norm(inputs, gains[0], shift_rows[0])
    normed_low = normed.astype(jnp.bfloat16)
    projected = jnp.dot(normed_low, qkv_w, preferred_element_type=jnp.float32)
    query = (projected[:, :D] + shift_rows[1]).astype(jnp.bfloat16)
    keyed = projected[:, D : 2 * D].astype(jnp.bfloat16)
    valued = (projected[:, 2 * D :] + shift_rows[2]).astype(jnp.bfloat16)
    query3 = query.reshape(tok_rows, H, DH)
    q_places, q_segment = row_places(position * tok_rows, tok_rows, deal_row, bounds, group_rows)

    def allowed_pairs(qp, qs, k_places, k_segment):
        return ((k_segment[None, :] == qs[:, None]) & (k_places[None, :] <= qp[:, None]))[None]

    initial = (
        jnp.full((H, tok_rows), -1e30, jnp.float32),
        jnp.zeros((H, tok_rows), jnp.float32),
        jnp.zeros((H, tok_rows, DH), jnp.float32),
    )
    key_rows = lax.all_gather(keyed, "ctx", axis=0, tiled=True)
    value_rows = lax.all_gather(valued, "ctx", axis=0, tiled=True)
    key_count = key_rows.shape[0]
    block_rows = 512
    block_count = key_count // block_rows
    k_places, k_segment = row_places(jnp.int32(0), key_count, deal_row, bounds, group_rows)
    stacked = (
        key_rows.reshape(block_count, block_rows, H, DH),
        value_rows.reshape(block_count, block_rows, H, DH),
        k_places.reshape(block_count, block_rows),
        k_segment.reshape(block_count, block_rows),
    )

    def visit_block(inner_state, pieces):
        maxima, totals, weighted = inner_state
        key3, value3, block_places, block_segment = pieces
        scores = (
            jnp.einsum("qhd,khd->hqk", query3, key3, preferred_element_type=jnp.float32) * scaling
        )
        allowed = allowed_pairs(q_places, q_segment, block_places, block_segment)
        masked = jnp.where(allowed, scores, -1e30)
        raised = jnp.maximum(maxima, jnp.max(masked, axis=-1))
        rescale = jnp.exp(maxima - raised)
        expo = jnp.where(allowed, jnp.exp(masked - raised[..., None]), 0.0)
        totals = totals * rescale + jnp.sum(expo, axis=-1)
        weighted = weighted * rescale[..., None] + jnp.einsum(
            "hqk,khd->hqd", expo.astype(jnp.bfloat16), value3, preferred_element_type=jnp.float32
        )
        return ((raised, totals, weighted), None)

    maxima, totals, weighted = lax.scan(visit_block, initial, stacked)[0]
    context3 = weighted / totals[..., None]
    log_total = maxima + jnp.log(totals)
    context = context3.transpose(1, 0, 2).reshape(tok_rows, D)
    inner = layer_norm(context, gains[1], shift_rows[3])
    inner_low = inner.astype(jnp.bfloat16)
    branch = jnp.dot(inner_low, out_w, preferred_element_type=jnp.float32) + shift_rows[4]
    middle = inputs + branch
    normed_two = layer_norm(middle, gains[2], shift_rows[5])
    normed_two_low = normed_two.astype(jnp.bfloat16)
    hidden = jnp.dot(normed_two_low, in_w, preferred_element_type=jnp.float32) + ffn_shift_rows[0]
    activated = gelu_exact(hidden)
    inner_two = layer_norm(activated, ffn_scale, ffn_shift_rows[1])
    inner_two_low = inner_two.astype(jnp.bfloat16)
    result = jnp.dot(inner_two_low, back_w, preferred_element_type=jnp.float32) + shift_rows[6]
    mixed_out = (middle + result).astype(jnp.bfloat16)
    loaded_back = (
        lax.all_gather(qkv_weight, "fsdp", axis=0, tiled=True),
        lax.all_gather(out_weight, "fsdp", axis=0, tiled=True),
        lax.all_gather(in_weight, "fsdp", axis=0, tiled=True),
        lax.all_gather(back_weight, "fsdp", axis=0, tiled=True),
        lax.all_gather(norm_gains, "fsdp", axis=1, tiled=True),
        lax.all_gather(shifts, "fsdp", axis=1, tiled=True),
        lax.all_gather(ffn_gain, "fsdp", axis=0, tiled=True),
        lax.all_gather(ffn_shifts, "fsdp", axis=1, tiled=True),
    )
    qkv_w, out_w, in_w, back_w, gains, shift_rows, ffn_scale, ffn_shift_rows = unpack(loaded_back)
    upstream = cotangent[0].astype(jnp.float32)
    result_low = cotangent[0]
    grad_back_w = outer_sum(inner_two_low, result_low)
    grad_back_bias = jnp.sum(result_low.astype(jnp.float32), axis=0)
    grad_inner_two = times_transposed(result_low, back_w)
    norm_pull = jax.vjp(layer_norm, activated, ffn_scale, ffn_shift_rows[1])[1]
    grad_activated, grad_ffn_gain, grad_ffn_shift = norm_pull(grad_inner_two)
    gelu_pull = jax.vjp(gelu_exact, hidden)[1]
    grad_hidden = gelu_pull(grad_activated)[0]
    hidden_low = grad_hidden.astype(jnp.bfloat16)
    grad_in_w = outer_sum(normed_two_low, hidden_low)
    grad_in_bias = jnp.sum(hidden_low.astype(jnp.float32), axis=0)
    grad_normed_two = times_transposed(hidden_low, in_w)
    second_pull = jax.vjp(layer_norm, middle, gains[2], shift_rows[5])[1]
    grad_middle_part, grad_gain_two, grad_shift_five = second_pull(grad_normed_two)
    grad_middle = upstream + grad_middle_part
    branch_low = grad_middle.astype(jnp.bfloat16)
    grad_out_w = outer_sum(inner_low, branch_low)
    grad_out_bias = jnp.sum(branch_low.astype(jnp.float32), axis=0)
    grad_inner = times_transposed(branch_low, out_w)
    inner_pull = jax.vjp(layer_norm, context, gains[1], shift_rows[3])[1]
    grad_context, grad_gain_one, grad_shift_three = inner_pull(grad_inner)
    context_grad_low = grad_context.astype(jnp.bfloat16).reshape(tok_rows, H, DH)
    delta = jnp.einsum("qhd,hqd->hq", context_grad_low.astype(jnp.float32), context3)

    def grad_pair(
        q_rows, grad_rows, lse_rows, delta_rows, qp, qs, key3, value3, k_places, k_segment
    ):
        scores = (
            jnp.einsum("qhd,khd->hqk", q_rows, key3, preferred_element_type=jnp.float32) * scaling
        )
        allowed = allowed_pairs(qp, qs, k_places, k_segment)
        probabilities = jnp.where(allowed, jnp.exp(scores - lse_rows[..., None]), 0.0)
        upstream_probs = jnp.einsum(
            "qhd,khd->hqk", grad_rows, value3, preferred_element_type=jnp.float32
        )
        score_grad = (probabilities * (upstream_probs - delta_rows[..., None])).astype(jnp.bfloat16)
        query_add = (
            jnp.einsum("hqk,khd->qhd", score_grad, key3, preferred_element_type=jnp.float32)
            * scaling
        )
        key_add = (
            jnp.einsum("hqk,qhd->khd", score_grad, q_rows, preferred_element_type=jnp.float32)
            * scaling
        )
        value_add = jnp.einsum(
            "hqk,qhd->khd",
            probabilities.astype(jnp.bfloat16),
            grad_rows,
            preferred_element_type=jnp.float32,
        )
        return (query_add, key_add, value_add)

    def grad_block(key3, value3, k_places, k_segment):
        return grad_pair(
            query3,
            context_grad_low,
            log_total,
            delta,
            q_places,
            q_segment,
            key3,
            value3,
            k_places,
            k_segment,
        )

    zero_query = jnp.zeros((tok_rows, H, DH), jnp.float32)
    gathered_keys, gathered_values = (
        lax.all_gather(keyed, "ctx", axis=0, tiled=True),
        lax.all_gather(valued, "ctx", axis=0, tiled=True),
    )
    stream_rows = gathered_keys.shape[0]
    block_rows = math.gcd(stream_rows, 512)
    block_count = stream_rows // block_rows
    all_places, all_segment = row_places(0, stream_rows, deal_row, bounds, group_rows)

    def sweep(query_grad, pieces):
        key3, value3, block_places, block_segment = pieces
        query_add, key_add, value_add = grad_block(key3, value3, block_places, block_segment)
        return (query_grad + query_add, (key_add, value_add))

    query_grad, (key_parts, value_parts) = lax.scan(
        sweep,
        zero_query,
        (
            gathered_keys.reshape(block_count, block_rows, H, DH),
            gathered_values.reshape(block_count, block_rows, H, DH),
            all_places.reshape(block_count, block_rows),
            all_segment.reshape(block_count, block_rows),
        ),
    )
    key_terms = key_parts.reshape(stream_rows, D)
    value_terms = value_parts.reshape(stream_rows, D)
    key_grad_mine, value_grad_mine = (
        lax.psum_scatter(
            key_terms.astype(jnp.bfloat16), "ctx", scatter_dimension=0, tiled=True
        ).astype(jnp.float32),
        lax.psum_scatter(
            value_terms.astype(jnp.bfloat16), "ctx", scatter_dimension=0, tiled=True
        ).astype(jnp.float32),
    )
    qkv_grad_low = jnp.concatenate(
        [query_grad.reshape(tok_rows, D), key_grad_mine, value_grad_mine], axis=1
    ).astype(jnp.bfloat16)
    grad_qkv_w = outer_sum(normed_low, qkv_grad_low)
    column_sums = jnp.sum(qkv_grad_low.astype(jnp.float32), axis=0)
    grad_query_bias = column_sums[:D]
    grad_value_bias = column_sums[2 * D :]
    grad_normed = times_transposed(qkv_grad_low, qkv_w)
    first_pull = jax.vjp(layer_norm, inputs, gains[0], shift_rows[0])[1]
    grad_inputs_part, grad_gain_zero, grad_shift_zero = first_pull(grad_normed)
    input_grad = grad_middle + grad_inputs_part
    gains_terms = jnp.stack([grad_gain_zero, grad_gain_one, grad_gain_two])
    shift_terms = jnp.stack(
        [
            grad_shift_zero,
            grad_query_bias,
            grad_value_bias,
            grad_shift_three,
            grad_out_bias,
            grad_shift_five,
            grad_back_bias,
        ]
    )
    ffn_shift_terms = jnp.stack([grad_in_bias, grad_ffn_shift])
    reduced = (
        lax.psum_scatter(grad_qkv_w, ("ctx", "fsdp"), scatter_dimension=0, tiled=True),
        lax.psum_scatter(grad_out_w, ("ctx", "fsdp"), scatter_dimension=0, tiled=True),
        lax.psum_scatter(grad_in_w, ("ctx", "fsdp"), scatter_dimension=0, tiled=True),
        lax.psum_scatter(grad_back_w, ("ctx", "fsdp"), scatter_dimension=0, tiled=True),
        lax.psum_scatter(gains_terms, ("ctx", "fsdp"), scatter_dimension=1, tiled=True),
        lax.psum_scatter(shift_terms, ("ctx", "fsdp"), scatter_dimension=1, tiled=True),
        lax.psum_scatter(grad_ffn_gain, ("ctx", "fsdp"), scatter_dimension=0, tiled=True),
        lax.psum_scatter(ffn_shift_terms, ("ctx", "fsdp"), scatter_dimension=1, tiled=True),
    )
    return (mixed_out[None], input_grad[None]) + tuple(reduced)


def solution(mesh):
    in_specs = (
        P("fsdp", "ctx", None),
        P("fsdp", "ctx", None),
        P("fsdp", None),
        P("fsdp", None),
        P("fsdp", None),
        P("fsdp", None),
        P("fsdp", None),
        P("fsdp", None),
        P(None, "fsdp"),
        P(None, "fsdp"),
        P("fsdp"),
        P(None, "fsdp"),
    )
    out_specs = (
        P("fsdp", "ctx", None),
        P("fsdp", "ctx", None),
        P(("ctx", "fsdp"), None),
        P(("ctx", "fsdp"), None),
        P(("ctx", "fsdp"), None),
        P(("ctx", "fsdp"), None),
        P(None, ("ctx", "fsdp")),
        P(None, ("ctx", "fsdp")),
        P(("ctx", "fsdp")),
        P(None, ("ctx", "fsdp")),
    )
    return jax.shard_map(local, mesh=mesh, in_specs=in_specs, out_specs=out_specs, check_vma=False)
```

profile of v0, /device:TPU:0, one launch (start us, length us, event | category | flops | bytes accessed | tf_op | source)
XLA Modules:
  0.0 1461.5 jit_solution(8794208688010352200)
XLA Ops:
  8.0 14.9 %all-gather.1 = bf16[4,192,7]{1,2,0:T(8,128)(2,1)S(1)} all-gather(bf16[1,192,7]{1,2,0:T(8,128)(2,1)} %bitcast.267), channel_id=1, replica_groups=mesh['ctx'=8,'fsdp'=4] {'fsdp'}, dimensions={0}, use_global_device_ids=true | all-gather | bytes 13440 | tf_op jit(solution)/shard_map/all_gather | solution.py:87
  23.0 12.2 all-gather
  38.9 43.6 %all-gather.10.cloned.1.call-done = bf16[768,2304]{1,0:T(8,128)(2,1)} async-done(((bf16[192,2304]{1,0:T(8,128)(2,1)}), bf16[768,2304]{1,0:T(8,128)(2,1)}) %all-gather.10.cloned.1.call-update) | async-done | bytes 3538960 | tf_op jit(solution)/shard_map/all_gather | solution.py:82
  95.8 13.0 all_gather.45
  109.5 13.6 all-gather.2
  124.2 10.1 all-gather.12.cloned.1.call-done
  134.3 8.6 copy.91
  142.9 7.5 copy.120
  155.3 26.5 %all-gather.14.cloned.1.call-done = bf16[4096,768]{1,0:T(8,128)(2,1)} async-done(((bf16[512,768]{1,0:T(8,128)(2,1)}), bf16[4096,768]{1,0:T(8,128)(2,1)}) %all-gather.14.cloned.1.call-update) | async-done | bytes 6291472 | tf_op jit(solution)/shard_map/all_gather | solution.py:111
  181.8 8.9 copy.93
  190.7 7.1 copy.121
  202.6 179.3 %while.30 = (s32[]{:T(128)}, f32[12,512]{1,0:T(8,128)S(1)}, f32[12,512]{1,0:T(8,128)S(1)}, f32[12,512,64]{1,2,0:T(8,128)}, s32[8,512]{1,0:T(8,128)S(1)}, /*index...) while((s32[]{:T(128)}, f32[12,512]{1,0:T(8,128)S(1)}, ...), condition=%wide.region_10.11_spmd.clone, body=%wide.region_7.10_spmd.clone.sunk | while | flops 848197632 | bytes 95043760 | solution.py:140
  202.9 8.0 fusion.150
  210.9 7.7 fusion.151
  225.0 8.0 fusion.150
  233.0 7.7 fusion.151
  247.4 8.0 fusion.150
  255.5 7.7 fusion.151
  269.9 8.0 fusion.150
  277.9 7.6 fusion.151
  292.3 8.0 fusion.150
  300.3 7.7 fusion.151
  314.7 8.0 fusion.150
  322.7 7.7 fusion.151
  337.1 8.0 fusion.150
  345.2 7.7 fusion.151
  359.6 8.0 fusion.150
  367.6 7.6 fusion.151
  389.9 21.5 %fusion.101 = (f32[512]{0:T(512)S(1)}, f32[512,3072]{1,0:T(8,128)}, f32[512,3072]{1,0:T(8,128)}, f32[512,3072]{1,0:T(8,128)}) fusion(f32[3072]{0:T(1024)S(1)} %bitcast.261, bf16[768,3072]{1,0:T(8,128)(2,1)} %all-gather.18.cloned.1.call-done, f32[512,768]{1,0:T(8,128)} %copy-done.10, f32[768]{0:T(1024)S(1)} %get-tuple-element.371, ...), kind=kOutput, calls=%fused_computation.205 | convolution fusion | flops 2521693696 | bytes 25190400 | tf_op jit(solution)/shard_map/dot_general | solution.py:150
  411.4 7.4 multiply_reduce_fusion.1
  422.2 10.8 convert_reduce_fusion
  434.6 6.0 multiply_reduce_fusion.3
  447.7 251.0 %while.31 = (s32[]{:T(128)}, f32[512,12,64]{0,2,1:T(8,128)}, bf16[8,512,12,64]{1,3,2,0:T(8,128)(2,1)}, bf16[8,512,12,64]{1,3,2,0:T(8,128)(2,1)}, bf16[8,512,12,6...) while((s32[]{:T(128)}, f32[512,12,64]{0,2,1:T(8,128)}, ...), condition=%wide.region_24.25_spmd.clone, body=%wide.region_23.24_spmd.clone.sunk | while | flops 2047082496 | bytes 195125520 | solution.py:249
  455.7 8.4 fusion.165
  486.7 8.4 fusion.165
  495.1 5.9 bitcast_add_fusion.2
  518.1 8.4 fusion.165
  526.5 5.9 bitcast_add_fusion.2
  549.4 8.4 fusion.165
  557.9 5.9 bitcast_add_fusion.2
  580.8 8.4 fusion.165
  589.3 5.9 bitcast_add_fusion.2
  612.1 8.4 fusion.165
  620.6 5.9 bitcast_add_fusion.2
  643.5 8.4 fusion.165
  652.0 5.9 bitcast_add_fusion.2
  674.9 8.4 fusion.165
  683.4 5.9 bitcast_add_fusion.2
  698.7 6.9 copy.101
  705.6 6.8 copy.123
  712.9 6.9 copy.100
  719.8 7.1 copy.122
  733.2 7.2 fusion.95
  742.3 6.2 fusion.66
  750.1 24.5 %reduce-scatter.14.cloned.1.call-done = bf16[512,768]{0,1:T(8,128)(2,1)} async-done(((bf16[4096,768]{0,1:T(8,128)(2,1)}), bf16[512,768]{0,1:T(8,128)(2,1)}) %reduce-scatter.14.cloned.1.call-update) | async-done | bytes 786448 | tf_op jit(solution)/shard_map/reduce_scatter | solution.py:265
  774.6 65.5 %reduce-scatter.12.cloned.1.call-done = bf16[512,768]{0,1:T(8,128)(2,1)} async-done(((bf16[4096,768]{0,1:T(8,128)(2,1)}), bf16[512,768]{0,1:T(8,128)(2,1)}) %reduce-scatter.12.cloned.1.call-update) | async-done | bytes 786448 | tf_op jit(solution)/shard_map/reduce_scatter | solution.py:262
  840.1 6.6 fusion.88
  848.2 6.8 fusion.64
  855.0 87.4 %reduce-scatter.24.cloned.1.call-done = f32[96,2]{1,0:T(8,128)} async-done(((f32[3072,2]{1,0:T(8,128)}), f32[96,2]{1,0:T(8,128)}) %reduce-scatter.24.cloned.1.call-update) | async-done | bytes 784
  952.3 40.7 %all-reduce.3 = (f32[3,768]{1,0:T(4,128)S(1)}, f32[7,768]{1,0:T(8,128)S(1)}, f32[3072]{0:T(1024)S(1)}) all-reduce(f32[3,768]{1,0:T(4,128)S(1)} %pad_maximum_fusion.2, f32[7,768]{1,0:T(8,128)S(1)} %stack.36, f32[3072]{0:T(1024)S(1)} %copy-done.25), channel_id=8, replica_groups=mesh['ctx'=8,'fsdp'=4] {'ctx','fsdp'}, use_global_device_ids=true, to_apply=%region_36.37.clone | all-reduce | flops 10752 | bytes 86016
  994.9 51.3 %reduce-scatter.18.cloned.1.call-done = f32[24,768]{1,0:T(8,128)} async-done(((f32[768,768]{1,0:T(8,128)}), f32[24,768]{1,0:T(8,128)}) %reduce-scatter.18.cloned.1.call-update) | async-done | bytes 73744 | tf_op jit(solution)/shard_map/reduce_scatter | solution.py:295
  1046.2 142.2 %reduce-scatter.20.cloned.1.call-done = f32[24,3072]{1,0:T(8,128)} async-done(((f32[768,3072]{1,0:T(8,128)}), f32[24,3072]{1,0:T(8,128)}) %reduce-scatter.20.cloned.1.call-update) | async-done | bytes 294928 | tf_op jit(solution)/shard_map/reduce_scatter | solution.py:296
  1188.4 140.8 %reduce-scatter.22.cloned.1.call-done = f32[96,768]{1,0:T(8,128)} async-done(((f32[3072,768]{1,0:T(8,128)}), f32[96,768]{1,0:T(8,128)}) %reduce-scatter.22.cloned.1.call-update) | async-done | bytes 294928 | tf_op jit(solution)/shard_map/reduce_scatter | solution.py:297
  1329.2 125.6 %reduce-scatter.16.cloned.1.call-done = f32[24,2304]{1,0:T(8,128)} async-done(((f32[768,2304]{1,0:T(8,128)}), f32[24,2304]{1,0:T(8,128)}) %reduce-scatter.16.cloned.1.call-update) | async-done | bytes 221200 | tf_op jit(solution)/shard_map/reduce_scatter | solution.py:294
  (371 shorter events, 267.5 us)
Async XLA Ops:
  7.2 75.3 %all-gather.10.cloned.1.call-start = ((), (), s32[]{:S(2)}) async-start(), calls=%async_computation.7 | async-start | bytes 4423680 | tf_op jit(solution)/shard_map/all_gather | solution.py:82
  7.9 126.4 %all-gather.12.cloned.1.call-start = ((), (), s32[]{:S(2)}) async-start(), calls=%async_computation.8 | async-start | bytes 7077888 | tf_op jit(solution)/shard_map/all_gather | solution.py:110
  35.4 51.5 %copy-start.26 = (f32[768]{0:T(1024)}, f32[768]{0:T(1024)S(1)}, u32[]{:S(2)}) copy-start(f32[768]{0:T(1024)S(1)} %get-tuple-element.379) | copy-start | bytes 9220
  36.0 50.9 %copy-start.39 = (f32[768]{0:T(1024)}, f32[768]{0:T(1024)S(1)}, u32[]{:S(2)}) copy-start(f32[768]{0:T(1024)S(1)} %get-tuple-element.376) | copy-start | bytes 9220
  36.0 349.6 %copy-start.43 = (f32[768]{0:T(1024)}, f32[768]{0:T(1024)S(1)}, u32[]{:S(2)}) copy-start(f32[768]{0:T(1024)S(1)} %get-tuple-element.373) | copy-start | bytes 9220
  36.0 353.9 %copy-start.41 = (f32[768]{0:T(1024)}, f32[768]{0:T(1024)S(1)}, u32[]{:S(2)}) copy-start(f32[768]{0:T(1024)S(1)} %get-tuple-element.371) | copy-start | bytes 9220
  37.3 49.5 %copy-start.28 = (f32[512]{0:T(512)}, f32[512]{0:T(512)S(1)}, u32[]{:S(2)}) copy-start(f32[512]{0:T(512)S(1)} %broadcast_multiply_fusion.4) | copy-start | bytes 6148
  38.8 48.0 %copy-start.32 = (f32[512]{0:T(512)}, f32[512]{0:T(512)S(1)}, u32[]{:S(2)}) copy-start(f32[512]{0:T(512)S(1)} %fusion.57) | copy-start | bytes 6148
  38.8 48.0 %copy-start.30 = (f32[512]{0:T(512)}, f32[512]{0:T(512)S(1)}, u32[]{:S(2)}) copy-start(f32[512]{0:T(512)S(1)} %fusion.83) | copy-start | bytes 6148
  90.1 5.0 copy-start.50
  90.1 5.2 copy-start.53
  90.1 5.7 copy-start.49
  90.1 19.4 %copy-start.51 = (bf16[768]{0:T(1024)(128)(2,1)S(1)}, bf16[768]{0:T(1024)(128)(2,1)}, u32[]{:S(2)}) copy-start(bf16[768]{0:T(1024)(128)(2,1)} %param.26) | copy-start | bytes 4612
  90.1 91.7 %all-gather.14.cloned.1.call-start = ((), (), s32[]{:S(2)}) async-start(), calls=%async_computation.9 | async-start | bytes 7077888 | tf_op jit(solution)/shard_map/all_gather | solution.py:111
  93.2 292.3 %all-gather.16.cloned.1.call-start = ((), (), s32[]{:S(2)}) async-start(), calls=%async_computation.10 | async-start | bytes 1474560 | tf_op jit(solution)/shard_map/all_gather | solution.py:83
  93.8 296.1 %all-gather.18.cloned.1.call-start = ((), (), s32[]{:S(2)}) async-start(), calls=%async_computation.11 | async-start | bytes 5898240 | tf_op jit(solution)/shard_map/all_gather | solution.py:84
  94.4 317.0 %all-gather.20.cloned.1.call-start = ((), (), s32[]{:S(2)}) async-start(), calls=%async_computation.12 | async-start | bytes 5898240 | tf_op jit(solution)/shard_map/all_gather | solution.py:85
  94.9 679.7 %reduce-scatter.14.cloned.1.call-start = ((), (), s32[]{:S(2)}) async-start(), calls=%async_computation.14 | async-start | bytes 7077888 | tf_op jit(solution)/shard_map/reduce_scatter | solution.py:265
  210.9 8.3 copy-start
  233.0 8.4 copy-start
  255.5 8.4 copy-start
  277.9 8.3 copy-start
  300.3 8.3 copy-start
  322.7 8.4 copy-start
  345.1 8.4 copy-start
  367.6 8.3 copy-start
  389.9 21.5 %copy-start.19 = (bf16[1,512,768]{2,1,0:T(8,128)(2,1)S(1)}, bf16[1,512,768]{2,1,0:T(8,128)(2,1)}, u32[]{:S(2)}) copy-start(bf16[1,512,768]{2,1,0:T(8,128)(2,1)} %param.17) | copy-start | bytes 2359300
  411.4 7.4 copy-start.5
  422.2 12.4 copy-start.11
  451.1 4.6 copy-start.2
  464.1 5.4 copy-start.1
  464.1 10.3 copy-start.3
  482.1 4.6 copy-start.2
  495.1 5.9 copy-start.1
  495.1 10.6 copy-start.3
  513.5 4.6 copy-start.2
  526.5 5.9 copy-start.1
  526.5 10.6 copy-start.3
  544.8 4.6 copy-start.2
  557.9 5.9 copy-start.1
  557.9 10.6 copy-start.3
  576.2 4.6 copy-start.2
  589.3 5.9 copy-start.1
  589.3 10.6 copy-start.3
  620.6 5.9 copy-start.1
  620.6 10.7 copy-start.3
  652.0 5.9 copy-start.1
  652.0 10.7 copy-start.3
  683.4 5.9 copy-start.1
  683.4 10.6 copy-start.3
  712.4 127.7 %reduce-scatter.12.cloned.1.call-start = ((), (), s32[]{:S(2)}) async-start(), calls=%async_computation.13 | async-start | bytes 7077888 | tf_op jit(solution)/shard_map/reduce_scatter | solution.py:262
  727.0 215.4 %reduce-scatter.24.cloned.1.call-start = ((), (), s32[]{:S(2)}) async-start(), calls=%async_computation.19 | async-start | bytes 1622016
  729.4 316.8 %reduce-scatter.18.cloned.1.call-start = ((), (), s32[]{:S(2)}) async-start(), calls=%async_computation.16 | async-start | bytes 2433024 | tf_op jit(solution)/shard_map/reduce_scatter | solution.py:295
  733.2 455.3 %reduce-scatter.20.cloned.1.call-start = ((), (), s32[]{:S(2)}) async-start(), calls=%async_computation.17 | async-start | bytes 9732096 | tf_op jit(solution)/shard_map/reduce_scatter | solution.py:296
  740.5 588.7 %reduce-scatter.22.cloned.1.call-start = ((), (), s32[]{:S(2)}) async-start(), calls=%async_computation.18 | async-start | bytes 9732096 | tf_op jit(solution)/shard_map/reduce_scatter | solution.py:297
  748.6 91.6 %copy-start.9 = (bf16[1,512,768]{2,1,0:T(8,128)(2,1)S(1)}, bf16[1,512,768]{2,1,0:T(8,128)(2,1)}, u32[]{:S(2)}) copy-start(bf16[1,512,768]{2,1,0:T(8,128)(2,1)} %param.16) | copy-start | bytes 2359300
  748.6 91.6 %copy-start.27 = (f32[768]{0:T(1024)S(1)}, f32[768]{0:T(1024)}, u32[]{:S(2)}) copy-start(f32[768]{0:T(1024)} %copy-done.26) | copy-start | bytes 9220
  748.6 91.6 %copy-start.29 = (f32[512]{0:T(512)S(1)}, f32[512]{0:T(512)}, u32[]{:S(2)}) copy-start(f32[512]{0:T(512)} %copy-done.28) | copy-start | bytes 6148
  748.6 91.6 %copy-start.31 = (f32[512]{0:T(512)S(1)}, f32[512]{0:T(512)}, u32[]{:S(2)}) copy-start(f32[512]{0:T(512)} %copy-done.30) | copy-start | bytes 6148
  748.6 91.6 %copy-start.40 = (f32[768]{0:T(1024)S(1)}, f32[768]{0:T(1024)}, u32[]{:S(2)}) copy-start(f32[768]{0:T(1024)} %copy-done.39) | copy-start | bytes 9220
  748.6 706.2 %reduce-scatter.16.cloned.1.call-start = ((), (), s32[]{:S(2)}) async-start(), calls=%async_computation.15 | async-start | bytes 7299072 | tf_op jit(solution)/shard_map/reduce_scatter | solution.py:294
  943.8 4.9 copy-start.33
  943.8 5.8 copy-start.21
  943.8 5.8 copy-start.23
  (31 other events, 69.5 us)
Sparse Core Ops, SparseCore 0:
  9.6 72.8 all-gather.9
  90.2 44.0 all-gather.11
  136.2 45.5 all-gather.13
  183.2 30.4 all-gather.15
  215.1 88.5 all-gather.17
  305.1 87.8 all-gather.19
  712.5 62.0 reduce-scatter.13
  778.4 61.7 reduce-scatter.11
  845.4 96.9 reduce-scatter.23
  948.1 98.0 reduce-scatter.17
  1053.7 134.6 reduce-scatter.19
  1194.8 134.4 reduce-scatter.21
  1336.4 118.3 reduce-scatter.15
where the time goes:
time: 1470 us; the launch traced here: 1460 us
  waiting for transfers between devices  720 us (49%)
  matrix products  403 us (27%)
  local copies, waits for them, and re-layouts  131 us (9%)
  other arithmetic  96.1 us (7%)
  blocking collectives  94.5 us (6%)
  between operations  14.9 us (1%)
    reduce_scatter x1, waiting for transfers between devices, local(): lax.psum_scatter(grad_in_w, ('ctx', 'fsdp'), scatter_dimension=0, tiled=T...  142 us
    reduce_scatter x1, waiting for transfers between devices, local(): lax.psum_scatter(grad_back_w, ('ctx', 'fsdp'), scatter_dimension=0, tiled...  141 us
    reduce_scatter x1, waiting for transfers between devices, local(): lax.psum_scatter(grad_qkv_w, ('ctx', 'fsdp'), scatter_dimension=0, tiled=...  126 us
    unnamed x14, waiting for transfers between devices  89.8 us
    dot_general x8, matrix products, grad_pair(): jnp.einsum('qhd,khd->hqk', grad_rows, value3, preferred_element_type=jnp....  67.5 us
    reduce_scatter x1, waiting for transfers between devices, local(): lax.psum_scatter(key_terms.astype(jnp.bfloat16), 'ctx', scatter_dimension...  65.5 us
    dot_general x8, matrix products, visit_block(): jnp.einsum('qhd,khd->hqk', query3, key3, preferred_element_type=jnp.float32)  64 us
    reduce_sum x8, other arithmetic, visit_block(): totals = totals * rescale + jnp.sum(expo, axis=-1)  61.3 us
  transfers between devices with their start and end apart: 13, of which 10 were waited for; matrix products, arithmetic and copies ran while one was open for 21% of the time, Pallas kernels for 0%

commit v1 on v0

--- a/solution.py
+++ b/solution.py
@@ -108,7 +108,16 @@
         jnp.zeros((H, tok_rows, DH), jnp.float32),
     )
     key_rows = lax.all_gather(keyed, "ctx", axis=0, tiled=True)
-    value_rows = lax.all_gather(valued, "ctx", axis=0, tiled=True)
+    ways = lax.axis_size("ctx")
+    up = [(d, (d + 1) % ways) for d in range(ways)]
+    down = [(d, (d - 1) % ways) for d in range(ways)]
+    earlier, later = ([valued], [valued])
+    for _ in range(ways // 2):
+        earlier.append(lax.ppermute(earlier[-1], "ctx", up))
+    for _ in range((ways - 1) // 2):
+        later.append(lax.ppermute(later[-1], "ctx", down))
+    line = jnp.concatenate([*earlier[::-1], *later[1:]], axis=0)
+    value_rows = jnp.roll(line, (lax.axis_index("ctx") - ways // 2) * valued.shape[0], axis=0)
     key_count = key_rows.shape[0]
     block_rows = 512
     block_count = key_count // block_rows

time: 1470 us -> 1550 us (1.054)
  waiting for transfers between devices: 720 us -> 755 us
  local copies, waits for them, and re-layouts: 131 us -> 163 us
    ppermute x0 -> x7, waiting for transfers between devices: none -> 69.7 us  [the longest x4 51.2 us: local(): earlier.append(lax.ppermute(earlier[-1], 'ctx', up))]
    all_gather x1, waiting for transfers between devices: 26.5 us -> 0.02 us  [local(): lax.all_gather(valued, 'ctx', axis=0, tiled=True)]
    unnamed x112 -> x141, local copies, waits for them, and re-layouts: 54 us -> 73.7 us
  transfers between devices with their start and end apart: 13 -> 20, of which waited for: 10 -> 12; matrix products, arithmetic and copies ran while one was open for 21% -> 22% of each run, Pallas kernels for 0% -> 0%
where the time goes in v1:
time: 1550 us; the launch traced here: 1540 us
  waiting for transfers between devices  755 us (49%)
  matrix products  406 us (26%)
  local copies, waits for them, and re-layouts  163 us (11%)
  other arithmetic  96.3 us (6%)
  blocking collectives  94.3 us (6%)
    reduce_scatter x1, waiting for transfers between devices, local(): lax.psum_scatter(grad_in_w, ('ctx', 'fsdp'), scatter_dimension=0, tiled=T...  142 us
    reduce_scatter x1, waiting for transfers between devices, local(): lax.psum_scatter(grad_back_w, ('ctx', 'fsdp'), scatter_dimension=0, tiled...  141 us
    reduce_scatter x1, waiting for transfers between devices, local(): lax.psum_scatter(grad_qkv_w, ('ctx', 'fsdp'), scatter_dimension=0, tiled=...  125 us
    unnamed x14, waiting for transfers between devices  90 us
    unnamed x141, local copies, waits for them, and re-layouts  73.7 us
    dot_general x8, matrix products, grad_pair(): jnp.einsum('qhd,khd->hqk', grad_rows, value3, preferred_element_type=jnp....  67.5 us
    reduce_scatter x1, waiting for transfers between devices, local(): lax.psum_scatter(key_terms.astype(jnp.bfloat16), 'ctx', scatter_dimension...  65.5 us
    dot_general x8, matrix products, visit_block(): jnp.einsum('qhd,khd->hqk', query3, key3, preferred_element_type=jnp.float32)  65.4 us
  transfers between devices with their start and end apart: 20, of which 12 were waited for; matrix products, arithmetic and copies ran while one was open for 22% of the time, Pallas kernels for 0%

profile of v1, /device:TPU:0, one launch (start us, length us, event | category | flops | bytes accessed | tf_op | source)
XLA Modules:
  0.0 1538.7 jit_solution(12226995607455905103)
XLA Ops:
  8.0 14.9 all-gather.1
  23.0 12.2 all-gather
  38.9 43.6 %all-gather.10.cloned.1.call-done = bf16[768,2304]{1,0:T(8,128)(2,1)} async-done(((bf16[192,2304]{1,0:T(8,128)(2,1)}), bf16[768,2304]{1,0:T(8,128)(2,1)}) %all-gather.10.cloned.1.call-update) | async-done | bytes 3538960 | tf_op jit(solution)/shard_map/all_gather | solution.py:82
  94.3 20.7 %collective-permute-done = bf16[512,768]{1,0:T(8,128)(2,1)S(1)} collective-permute-done((bf16[512,768]{1,0:T(8,128)(2,1)S(1)}, bf16[512,768]{1,0:T(8,128)(2,1)S(1)}, u32[]{:S(2)}, u32[]{:S(2)}) %collective-permute-start) | collective-permute-done | bytes 786464 | tf_op jit(solution)/shard_map/ppermute | solution.py:116
  118.0 30.4 %collective-permute-done.1 = bf16[512,768]{1,0:T(8,128)(2,1)S(1)} collective-permute-done((bf16[512,768]{1,0:T(8,128)(2,1)S(1)}, bf16[512,768]{1,0:T(8,128)(2,1)S(1)}, u32[]{:S(2)}, u32[]{:S(2)}) %collective-permute-start.1) | collective-permute-done | bytes 786464 | tf_op jit(solution)/shard_map/ppermute | solution.py:116
  148.6 13.0 all-gather.2
  162.3 13.3 all_gather.43
  178.2 13.8 collective-permute-done.5
  212.9 8.6 copy.95
  221.6 7.0 copy.124
  233.5 8.8 copy.93
  242.3 7.0 copy.123
  254.1 181.0 %while.30 = (s32[]{:T(128)}, f32[12,512]{1,0:T(8,128)S(1)}, f32[12,512]{1,0:T(8,128)S(1)}, f32[12,512,64]{1,2,0:T(8,128)}, s32[8,512]{1,0:T(8,128)S(1)}, /*index...) while((s32[]{:T(128)}, f32[12,512]{1,0:T(8,128)S(1)}, ...), condition=%wide.region_10.11_spmd.clone, body=%wide.region_7.10_spmd.clone.sunk | while | flops 848197632 | bytes 95043760 | solution.py:149
  254.4 8.0 fusion.150
  262.4 7.7 fusion.151
  276.5 8.6 fusion.150
  285.1 7.6 fusion.151
  299.7 8.0 fusion.150
  307.7 7.7 fusion.151
  322.2 8.0 fusion.150
  330.2 7.7 fusion.151
  344.6 8.0 fusion.150
  352.6 7.7 fusion.151
  366.9 8.4 fusion.150
  375.4 7.7 fusion.151
  389.7 8.4 fusion.150
  398.1 7.8 fusion.151
  412.7 8.0 fusion.150
  420.7 7.7 fusion.151
  443.1 21.6 %fusion.101 = (f32[512]{0:T(512)S(1)}, f32[512,3072]{1,0:T(8,128)}, f32[512,3072]{1,0:T(8,128)}, f32[512,3072]{1,0:T(8,128)}) fusion(f32[3072]{0:T(1024)S(1)} %bitcast.270, bf16[768,3072]{1,0:T(8,128)(2,1)} %all-gather.16.cloned.1.call-done, f32[512,768]{1,0:T(8,128)} %copy-done.13, f32[768]{0:T(1024)S(1)} %get-tuple-element.371, ...), kind=kOutput, calls=%fused_computation.222 | convolution fusion | flops 2521693696 | bytes 25190400 | tf_op jit(solution)/shard_map/dot_general | solution.py:159
  464.7 7.4 multiply_reduce_fusion.1
  475.3 8.9 copy.99
  484.2 7.1 copy.125
  496.4 11.4 convert_reduce_fusion
  507.8 7.1 multiply_reduce_fusion.3
  522.1 251.5 %while.31 = (s32[]{:T(128)}, f32[512,12,64]{0,2,1:T(8,128)}, bf16[8,512,12,64]{1,3,2,0:T(8,128)(2,1)}, bf16[8,512,12,64]{1,3,2,0:T(8,128)(2,1)}, bf16[8,512,12,6...) while((s32[]{:T(128)}, f32[512,12,64]{0,2,1:T(8,128)}, ...), condition=%wide.region_24.25_spmd.clone, body=%wide.region_23.24_spmd.clone.sunk | while | flops 2047082496 | bytes 195125520 | solution.py:258
  530.2 8.4 fusion.165
  561.2 8.4 fusion.165
  569.6 5.9 bitcast_add_fusion.2
  592.6 8.4 fusion.165
  623.9 8.4 fusion.165
  632.4 5.9 bitcast_add_fusion.2
  655.3 8.4 fusion.165
  663.8 5.9 bitcast_add_fusion.2
  686.7 8.4 fusion.165
  695.2 5.9 bitcast_add_fusion.2
  718.1 8.4 fusion.165
  749.6 8.4 fusion.165
  773.6 6.9 copy.104
  780.6 6.9 copy.127
  787.7 6.9 copy.103
  794.6 7.2 copy.126
  808.1 7.5 fusion.95
  817.5 6.2 fusion.66
  825.2 26.7 %reduce-scatter.14.cloned.1.call-done = bf16[512,768]{0,1:T(8,128)(2,1)} async-done(((bf16[4096,768]{0,1:T(8,128)(2,1)}), bf16[512,768]{0,1:T(8,128)(2,1)}) %reduce-scatter.14.cloned.1.call-update) | async-done | bytes 786448 | tf_op jit(solution)/shard_map/reduce_scatter | solution.py:274
  851.9 65.5 %reduce-scatter.12.cloned.1.call-done = bf16[512,768]{0,1:T(8,128)(2,1)} async-done(((bf16[4096,768]{0,1:T(8,128)(2,1)}), bf16[512,768]{0,1:T(8,128)(2,1)}) %reduce-scatter.12.cloned.1.call-update) | async-done | bytes 786448 | tf_op jit(solution)/shard_map/reduce_scatter | solution.py:271
  917.4 6.6 fusion.88
  925.5 6.8 fusion.64
  932.3 87.4 %reduce-scatter.24.cloned.1.call-done = f32[96,2]{1,0:T(8,128)} async-done(((f32[3072,2]{1,0:T(8,128)}), f32[96,2]{1,0:T(8,128)}) %reduce-scatter.24.cloned.1.call-update) | async-done | bytes 784
  1029.4 40.8 %all-reduce.3 = (f32[3,768]{1,0:T(4,128)S(1)}, f32[7,768]{1,0:T(8,128)S(1)}, f32[3072]{0:T(1024)S(1)}) all-reduce(f32[3,768]{1,0:T(4,128)S(1)} %pad_maximum_fusion.2, f32[7,768]{1,0:T(8,128)S(1)} %stack.36, f32[3072]{0:T(1024)S(1)} %copy-done.29), channel_id=8, replica_groups=mesh['ctx'=8,'fsdp'=4] {'ctx','fsdp'}, use_global_device_ids=true, to_apply=%region_36.37.clone | all-reduce | flops 10752 | bytes 86016
  1072.1 51.4 %reduce-scatter.18.cloned.1.call-done = f32[24,768]{1,0:T(8,128)} async-done(((f32[768,768]{1,0:T(8,128)}), f32[24,768]{1,0:T(8,128)}) %reduce-scatter.18.cloned.1.call-update) | async-done | bytes 73744 | tf_op jit(solution)/shard_map/reduce_scatter | solution.py:304
  1123.5 142.1 %reduce-scatter.20.cloned.1.call-done = f32[24,3072]{1,0:T(8,128)} async-done(((f32[768,3072]{1,0:T(8,128)}), f32[24,3072]{1,0:T(8,128)}) %reduce-scatter.20.cloned.1.call-update) | async-done | bytes 294928 | tf_op jit(solution)/shard_map/reduce_scatter | solution.py:305
  1265.6 141.0 %reduce-scatter.22.cloned.1.call-done = f32[96,768]{1,0:T(8,128)} async-done(((f32[3072,768]{1,0:T(8,128)}), f32[96,768]{1,0:T(8,128)}) %reduce-scatter.22.cloned.1.call-update) | async-done | bytes 294928 | tf_op jit(solution)/shard_map/reduce_scatter | solution.py:306
  1406.6 125.3 %reduce-scatter.16.cloned.1.call-done = f32[24,2304]{1,0:T(8,128)} async-done(((f32[768,2304]{1,0:T(8,128)}), f32[24,2304]{1,0:T(8,128)}) %reduce-scatter.16.cloned.1.call-update) | async-done | bytes 221200 | tf_op jit(solution)/shard_map/reduce_scatter | solution.py:303
  (418 shorter events, 311.8 us)
Async XLA Ops:
  7.2 75.3 %all-gather.10.cloned.1.call-start = ((), (), s32[]{:S(2)}) async-start(), calls=%async_computation.7 | async-start | bytes 4423680 | tf_op jit(solution)/shard_map/all_gather | solution.py:82
  7.9 225.6 %all-gather.12.cloned.1.call-start = ((), (), s32[]{:S(2)}) async-start(), calls=%async_computation.8 | async-start | bytes 7077888 | tf_op jit(solution)/shard_map/all_gather | solution.py:110
  35.4 51.5 %copy-start.30 = (f32[768]{0:T(1024)}, f32[768]{0:T(1024)S(1)}, u32[]{:S(2)}) copy-start(f32[768]{0:T(1024)S(1)} %get-tuple-element.379) | copy-start | bytes 9220
  36.0 50.9 %copy-start.43 = (f32[768]{0:T(1024)}, f32[768]{0:T(1024)S(1)}, u32[]{:S(2)}) copy-start(f32[768]{0:T(1024)S(1)} %get-tuple-element.376) | copy-start | bytes 9220
  36.0 402.8 %copy-start.47 = (f32[768]{0:T(1024)}, f32[768]{0:T(1024)S(1)}, u32[]{:S(2)}) copy-start(f32[768]{0:T(1024)S(1)} %get-tuple-element.373) | copy-start | bytes 9220
  36.0 407.1 %copy-start.45 = (f32[768]{0:T(1024)}, f32[768]{0:T(1024)S(1)}, u32[]{:S(2)}) copy-start(f32[768]{0:T(1024)S(1)} %get-tuple-element.371) | copy-start | bytes 9220
  37.3 49.5 %copy-start.32 = (f32[512]{0:T(512)}, f32[512]{0:T(512)S(1)}, u32[]{:S(2)}) copy-start(f32[512]{0:T(512)S(1)} %broadcast_multiply_fusion.4) | copy-start | bytes 6148
  38.8 48.0 %copy-start.36 = (f32[512]{0:T(512)}, f32[512]{0:T(512)S(1)}, u32[]{:S(2)}) copy-start(f32[512]{0:T(512)S(1)} %fusion.57) | copy-start | bytes 6148
  38.8 48.0 %copy-start.34 = (f32[512]{0:T(512)}, f32[512]{0:T(512)S(1)}, u32[]{:S(2)}) copy-start(f32[512]{0:T(512)S(1)} %fusion.83) | copy-start | bytes 6148
  89.1 25.9 %copy-start.57 = (s32[1,4]{1,0:T(1,128)S(1)}, s32[1,4]{1,0:T(1,128)}, u32[]{:S(2)}) copy-start(s32[1,4]{1,0:T(1,128)} %param.18) | copy-start | bytes 52
  89.1 26.1 %copy-start.54 = (s32[1,16]{1,0:T(1,128)S(1)}, s32[1,16]{1,0:T(1,128)}, u32[]{:S(2)}) copy-start(s32[1,16]{1,0:T(1,128)} %param.19) | copy-start | bytes 196
  89.1 59.5 %copy-start.55 = (bf16[768]{0:T(1024)(128)(2,1)S(1)}, bf16[768]{0:T(1024)(128)(2,1)}, u32[]{:S(2)}) copy-start(bf16[768]{0:T(1024)(128)(2,1)} %param.26) | copy-start | bytes 4612
  89.1 73.2 %copy-start.53 = (bf16[2,768]{1,0:T(2,128)(2,1)S(1)}, bf16[2,768]{1,0:T(2,128)(2,1)}, u32[]{:S(2)}) copy-start(bf16[2,768]{1,0:T(2,128)(2,1)} %param.27) | copy-start | bytes 9220
  90.1 348.7 %all-gather.14.cloned.1.call-start = ((), (), s32[]{:S(2)}) async-start(), calls=%async_computation.9 | async-start | bytes 1474560 | tf_op jit(solution)/shard_map/all_gather | solution.py:83
  90.8 352.2 %all-gather.16.cloned.1.call-start = ((), (), s32[]{:S(2)}) async-start(), calls=%async_computation.10 | async-start | bytes 5898240 | tf_op jit(solution)/shard_map/all_gather | solution.py:84
  91.4 373.3 %all-gather.18.cloned.1.call-start = ((), (), s32[]{:S(2)}) async-start(), calls=%async_computation.11 | async-start | bytes 5898240 | tf_op jit(solution)/shard_map/all_gather | solution.py:85
  92.0 383.3 %all-gather.20.cloned.1.call-start = ((), (), s32[]{:S(2)}) async-start(), calls=%async_computation.12 | async-start | bytes 7077888 | tf_op jit(solution)/shard_map/all_gather | solution.py:246
  94.2 84.0 %copy-start.9 = (bf16[512,768]{1,0:T(8,128)(2,1)}, bf16[512,768]{1,0:T(8,128)(2,1)S(1)}, u32[]{:S(2)}) copy-start(bf16[512,768]{1,0:T(8,128)(2,1)S(1)} %get-tuple-element.455) | copy-start | bytes 2359300
  94.2 20.8 %collective-permute-start = (bf16[512,768]{1,0:T(8,128)(2,1)S(1)}, bf16[512,768]{1,0:T(8,128)(2,1)S(1)}, u32[]{:S(2)}, u32[]{:S(2)}) collective-permute-start(bf16[512,768]{1,0:T(8,128)(2,1)S(1)} %get-tuple-element.455), channel_id=1, source_target_pairs={{0,4},{4,8},{8,12},{12,16},{16,20},{20,24},{24,28},{28,0},{1,5},{5... | collective-permute-start | bytes 2359304 | tf_op jit(solution)/shard_map/ppermute | solution.py:116
  115.0 33.5 %collective-permute-start.1 = (bf16[512,768]{1,0:T(8,128)(2,1)S(1)}, bf16[512,768]{1,0:T(8,128)(2,1)S(1)}, u32[]{:S(2)}, u32[]{:S(2)}) collective-permute-start(bf16[512,768]{1,0:T(8,128)(2,1)S(1)} %collective-permute-done), channel_id=1, source_target_pairs={{0,4},{4,8},{8,12},{12,16},{16,20},{20,24},{24,28},{28,0},{1,5},{5... | collective-permute-start | bytes 2359304 | tf_op jit(solution)/shard_map/ppermute | solution.py:116
  115.3 60.4 %collective-permute-start.4 = (bf16[512,768]{1,0:T(8,128)(2,1)S(1)}, bf16[512,768]{1,0:T(8,128)(2,1)}, u32[]{:S(2)}, u32[]{:S(2)}) collective-permute-start(bf16[512,768]{1,0:T(8,128)(2,1)S(1)} %get-tuple-element.455), channel_id=1, source_target_pairs={{0,28},{4,0},{8,4},{12,8},{16,12},{20,16},{24,20},{28,24},{1,29},{... | collective-permute-start | bytes 2359304 | tf_op jit(solution)/shard_map/ppermute | solution.py:118
  148.4 27.3 %collective-permute-start.2 = (bf16[512,768]{1,0:T(8,128)(2,1)S(1)}, bf16[512,768]{1,0:T(8,128)(2,1)}, u32[]{:S(2)}, u32[]{:S(2)}) collective-permute-start(bf16[512,768]{1,0:T(8,128)(2,1)S(1)} %collective-permute-done.1), channel_id=1, source_target_pairs={{0,4},{4,8},{8,12},{12,16},{16,20},{20,24},{24,28},{28,0},{1,5},{5... | collective-permute-start | bytes 2359304 | tf_op jit(solution)/shard_map/ppermute | solution.py:116
  175.7 16.3 %collective-permute-start.5 = (bf16[512,768]{1,0:T(8,128)(2,1)}, bf16[512,768]{1,0:T(8,128)(2,1)}, u32[]{:S(2)}, u32[]{:S(2)}) collective-permute-start(bf16[512,768]{1,0:T(8,128)(2,1)} %collective-permute-done.4), channel_id=1, source_target_pairs={{0,28},{4,0},{8,4},{12,8},{16,12},{20,16},{24,20},{28,24},{1,29},{... | collective-permute-start | bytes 2359304 | tf_op jit(solution)/shard_map/ppermute | solution.py:118
  175.8 19.2 %collective-permute-start.3 = (bf16[512,768]{1,0:T(8,128)(2,1)}, bf16[512,768]{1,0:T(8,128)(2,1)}, u32[]{:S(2)}, u32[]{:S(2)}) collective-permute-start(bf16[512,768]{1,0:T(8,128)(2,1)} %collective-permute-done.2), channel_id=1, source_target_pairs={{0,4},{4,8},{8,12},{12,16},{16,20},{20,24},{24,28},{28,0},{1,5},{5... | collective-permute-start | bytes 2359304 | tf_op jit(solution)/shard_map/ppermute | solution.py:116
  178.2 19.4 %copy-start.10 = (bf16[512,768]{1,0:T(8,128)(2,1)S(1)}, bf16[512,768]{1,0:T(8,128)(2,1)}, u32[]{:S(2)}) copy-start(bf16[512,768]{1,0:T(8,128)(2,1)} %copy-done.9) | copy-start | bytes 2359300
  178.2 673.7 %reduce-scatter.14.cloned.1.call-start = ((), (), s32[]{:S(2)}) async-start(), calls=%async_computation.14 | async-start | bytes 7077888 | tf_op jit(solution)/shard_map/reduce_scatter | solution.py:274
  192.0 12.8 collective-permute-start.6
  262.4 8.3 copy-start
  285.1 8.5 copy-start
  307.7 8.4 copy-start
  330.2 8.4 copy-start
  352.6 8.3 copy-start
  375.4 8.3 copy-start
  398.1 8.6 copy-start
  420.7 8.3 copy-start
  443.1 21.6 %copy-start.22 = (bf16[1,512,768]{2,1,0:T(8,128)(2,1)S(1)}, bf16[1,512,768]{2,1,0:T(8,128)(2,1)}, u32[]{:S(2)}) copy-start(bf16[1,512,768]{2,1,0:T(8,128)(2,1)} %param.17) | copy-start | bytes 2359300
  443.1 21.6 %copy-start.27 = (f32[4,1,768]{2,1,0:T(1,128)S(1)}, f32[4,1,768]{2,1,0:T(1,128)}, u32[]{:S(2)}) copy-start(f32[4,1,768]{2,1,0:T(1,128)} %convert_element_type.127) | copy-start | bytes 36868
  464.7 7.4 copy-start.5
  484.2 12.1 slice-start
  496.4 11.4 copy-start.14
  507.8 7.1 copy-start.21
  538.6 10.3 copy-start.3
  569.6 10.7 copy-start.3
  601.0 10.7 copy-start.3
  632.4 10.7 copy-start.3
  663.8 10.7 copy-start.3
  695.2 10.7 copy-start.3
  726.6 10.7 copy-start.3
  758.0 10.7 copy-start.3
  787.5 129.9 %reduce-scatter.12.cloned.1.call-start = ((), (), s32[]{:S(2)}) async-start(), calls=%async_computation.13 | async-start | bytes 7077888 | tf_op jit(solution)/shard_map/reduce_scatter | solution.py:271
  801.9 6.2 copy-start.15
  801.9 217.8 %reduce-scatter.24.cloned.1.call-start = ((), (), s32[]{:S(2)}) async-start(), calls=%async_computation.19 | async-start | bytes 1622016
  804.3 319.2 %reduce-scatter.18.cloned.1.call-start = ((), (), s32[]{:S(2)}) async-start(), calls=%async_computation.16 | async-start | bytes 2433024 | tf_op jit(solution)/shard_map/reduce_scatter | solution.py:304
  808.0 457.6 %reduce-scatter.20.cloned.1.call-start = ((), (), s32[]{:S(2)}) async-start(), calls=%async_computation.17 | async-start | bytes 9732096 | tf_op jit(solution)/shard_map/reduce_scatter | solution.py:305
  815.6 591.0 %reduce-scatter.22.cloned.1.call-start = ((), (), s32[]{:S(2)}) async-start(), calls=%async_computation.18 | async-start | bytes 9732096 | tf_op jit(solution)/shard_map/reduce_scatter | solution.py:306
  823.7 93.7 %copy-start.12 = (bf16[1,512,768]{2,1,0:T(8,128)(2,1)S(1)}, bf16[1,512,768]{2,1,0:T(8,128)(2,1)}, u32[]{:S(2)}) copy-start(bf16[1,512,768]{2,1,0:T(8,128)(2,1)} %param.16) | copy-start | bytes 2359300
  823.7 93.7 %copy-start.31 = (f32[768]{0:T(1024)S(1)}, f32[768]{0:T(1024)}, u32[]{:S(2)}) copy-start(f32[768]{0:T(1024)} %copy-done.30) | copy-start | bytes 9220
  823.7 93.7 %copy-start.33 = (f32[512]{0:T(512)S(1)}, f32[512]{0:T(512)}, u32[]{:S(2)}) copy-start(f32[512]{0:T(512)} %copy-done.32) | copy-start | bytes 6148
  823.7 93.7 %copy-start.35 = (f32[512]{0:T(512)S(1)}, f32[512]{0:T(512)}, u32[]{:S(2)}) copy-start(f32[512]{0:T(512)} %copy-done.34) | copy-start | bytes 6148
  823.7 93.7 %copy-start.44 = (f32[768]{0:T(1024)S(1)}, f32[768]{0:T(1024)}, u32[]{:S(2)}) copy-start(f32[768]{0:T(1024)} %copy-done.43) | copy-start | bytes 9220
  823.8 708.1 %reduce-scatter.16.cloned.1.call-start = ((), (), s32[]{:S(2)}) async-start(), calls=%async_computation.15 | async-start | bytes 7299072 | tf_op jit(solution)/shard_map/reduce_scatter | solution.py:303
  1021.1 6.3 copy-start.8
  1021.1 6.3 copy-start.23
  1021.1 6.3 copy-start.39
  (44 other events, 158.5 us)
Sparse Core Ops, SparseCore 0:
  9.6 72.8 all-gather.9
  90.2 63.9 all-gather.11
  155.8 29.3 all-gather.13
  186.6 88.9 all-gather.15
  277.0 87.8 all-gather.17
  366.6 43.9 all-gather.19
  787.6 64.2 reduce-scatter.13
  855.6 61.7 reduce-scatter.11
  922.7 96.9 reduce-scatter.23
  1025.4 98.0 reduce-scatter.17
  1131.0 134.5 reduce-scatter.19
  1271.9 134.5 reduce-scatter.21
  1413.8 118.0 reduce-scatter.15
